TPU v7x, 32 devices: a whole 2x2x4 slice. The times are simulated.
32 devices in a mesh: fsdp: 8 (over z, x), tp: 4 (over y, core).
Axes of the slice: x: 2, y: 2, z: 4, core: 2. Of those that a mesh axis runs over, the one named last changes fastest.
Arguments:
- tokens: bfloat16 [8, 2048, 768], P('fsdp', 'tp'), may hold values from -6 to 6
- lengths: int32 [8, 4], P('fsdp'), may hold values from 288 to 1024, as said below
- pictures: int32 [8, 2048], P('fsdp'), may hold values from 0 to 3, as said below
- w_query: bfloat16 [768, 768], P('fsdp', 'tp'), may hold values from -0.21875 to 0.21875
- w_key: bfloat16 [768, 768], P('fsdp', 'tp'), may hold values from -0.21875 to 0.21875
- w_value: bfloat16 [768, 768], P('fsdp', 'tp'), may hold values from -0.21875 to 0.21875
- w_out: bfloat16 [768, 768], P('tp', 'fsdp'), may hold values from -0.875 to 0.875
- w_up: bfloat16 [768, 3072], P('fsdp', 'tp'), may hold values from -0.21875 to 0.21875
- w_down: bfloat16 [3072, 768], P('tp', 'fsdp'), may hold values from -0.15625 to 0.15625
- norm1_gain: float32 [768], P(('fsdp', 'tp')), may hold values from 0.5 to 1.5
- norm1_shift: float32 [768], P(('fsdp', 'tp')), may hold values from -1.75 to 1.75
- norm2_gain: float32 [768], P(('fsdp', 'tp')), may hold values from 0.5 to 1.5
- norm2_shift: float32 [768], P(('fsdp', 'tp')), may hold values from -1.75 to 1.75
- query_gain: float32 [768], P(('fsdp', 'tp')), may hold values from 1 to 2
- key_gain: float32 [768], P(('fsdp', 'tp')), may hold values from 1 to 2
- cotangent: bfloat16 [8, 2048, 768], P('fsdp', 'tp'), may hold values from -6 to 6
Outputs:
- layer_out: bfloat16 [8, 2048, 768], P('fsdp', 'tp')
- input_grad: float32 [8, 2048, 768], P('fsdp', 'tp')
- grad_query: float32 [768, 768], P('fsdp', 'tp')
- grad_key: float32 [768, 768], P('fsdp', 'tp')
- grad_value: float32 [768, 768], P('fsdp', 'tp')
- grad_output_proj: float32 [768, 768], P('tp', 'fsdp')
- grad_up: float32 [768, 3072], P('fsdp', 'tp')
- grad_down: float32 [3072, 768], P('tp', 'fsdp')
- grad_norm1_gain: float32 [768], P(('fsdp', 'tp'))
- grad_norm1_shift: float32 [768], P(('fsdp', 'tp'))
- grad_norm2_gain: float32 [768], P(('fsdp', 'tp'))
- grad_norm2_shift: float32 [768], P(('fsdp', 'tp'))
- grad_query_gain: float32 [768], P(('fsdp', 'tp'))
- grad_key_gain: float32 [768], P(('fsdp', 'tp'))
- statistics: float32 [4], replicated
Inputs may be any that keep to these rules, and one draw needn't show every extreme that they name: The lengths of a row sum to at most 2048; one picture of every row has exactly 1024 patches. Slots of a row carry the pictures in order, each picture covering as many slots as its length; slots after the row's total length repeat the last picture's number.
All inputs are finite; a program needn't handle non-finite values.
Results may differ from a plain program's by a relative error of at most 0.018.
Values may be sent and summed in bfloat16 or wider, within the bound.
A program may use at most 192 MiB of HBM per device.

v0:
```python
import jax
import jax.numpy as jnp
from jax import lax
from jax.sharding import PartitionSpec as P

HD = 64


EPS = 1e-06
ROOT_HALF = 0.7071067811865476
DENSITY = 0.3989422804014327


def normalise(values, scaling, offset):
    centre = jnp.mean(values, axis=-1, keepdims=True)
    centred = values - centre
    spread = jnp.mean(centred * centred, axis=-1, keepdims=True)
    inverse = lax.rsqrt(spread + EPS)
    normed = centred * inverse
    return (normed * scaling + offset, normed, inverse)


def normalise_back(grad_out, normed, inverse, scaling):
    grad_unit = grad_out * scaling
    grad_values = inverse * (
        grad_unit
        - jnp.mean(grad_unit, axis=-1, keepdims=True)
        - normed * jnp.mean(grad_unit * normed, axis=-1, keepdims=True)
    )
    return (grad_values, jnp.sum(grad_out * normed, axis=(0, 1)), jnp.sum(grad_out, axis=(0, 1)))


def gelu_slope(values):
    return (
        0.5 * (1.0 + jax.scipy.special.erf(values * ROOT_HALF))
        + values * jnp.exp(-0.5 * values * values) * DENSITY
    )


def gather_tokens(values):
    return lax.all_gather(values, "tp", axis=1, tiled=True)


def gather_grads(values):
    return lax.all_gather(values, "tp", axis=1, tiled=True)


def reduce_tokens(values):
    return lax.psum_scatter(
        values.astype(jnp.bfloat16), "tp", scatter_dimension=1, tiled=True
    ).astype(jnp.float32)


def reduce_grads(values):
    return lax.psum_scatter(
        values.astype(jnp.bfloat16), "tp", scatter_dimension=1, tiled=True
    ).astype(jnp.float32)


def block_scores(query, keyed, picture_query, picture_key, key_mask):
    raw_scores = jnp.einsum("qhd,khd->hqk", query, keyed, preferred_element_type=jnp.float32)
    allowed = (picture_query[:, None] == picture_key[None, :]) & (key_mask[None, :] > 0)
    return jnp.where(allowed[None], raw_scores * query.shape[-1] ** (-0.5), -1e30)


def forward_row(packed):
    query_row, key_row, value_row, picture_row, mask_row = packed
    full_len = query_row.shape[0]
    block_len = min(512, full_len)
    block_count = full_len // block_len

    def forward_one_block(packed_block):
        query_block, picture_block = packed_block
        scores = block_scores(query_block, key_row, picture_block, picture_row, mask_row)
        highest = jnp.max(scores, axis=-1, keepdims=True)
        logsum = highest + jnp.log(jnp.sum(jnp.exp(scores - highest), axis=-1, keepdims=True))
        probability = jnp.exp(scores - logsum).astype(jnp.bfloat16)
        mixture = jnp.einsum(
            "hqk,khd->qhd", probability, value_row, preferred_element_type=jnp.float32
        )
        return (mixture, logsum)

    query_blocks = query_row.reshape((block_count, block_len) + query_row.shape[1:])
    return lax.map(forward_one_block, (query_blocks, picture_row.reshape(block_count, block_len)))


def backward_row(packed):
    query_row, key_row, value_row, picture_row, mask_row, grad_row, logsum_row = packed
    full_len = query_row.shape[0]
    block_len = min(512, full_len)
    block_count = full_len // block_len
    factor = query_row.shape[-1] ** (-0.5)

    def backward_one_block(running, packed_block):
        grad_key, grad_value = running
        query_block, picture_block, grad_block, logsum_block = packed_block
        scores = block_scores(query_block, key_row, picture_block, picture_row, mask_row)
        probability = jnp.exp(scores - logsum_block)
        prob_low = probability.astype(jnp.bfloat16)
        grad_prob = jnp.einsum(
            "qhd,khd->hqk", grad_block, value_row, preferred_element_type=jnp.float32
        )
        grad_value = grad_value + jnp.einsum(
            "hqk,qhd->khd", prob_low, grad_block, preferred_element_type=jnp.float32
        )
        centre = jnp.sum(probability * grad_prob, axis=-1, keepdims=True)
        grad_scores = (probability * (grad_prob - centre)).astype(jnp.bfloat16)
        grad_query = factor * jnp.einsum(
            "hqk,khd->qhd", grad_scores, key_row, preferred_element_type=jnp.float32
        )
        grad_key = grad_key + factor * jnp.einsum(
            "hqk,qhd->khd", grad_scores, query_block, preferred_element_type=jnp.float32
        )
        return ((grad_key, grad_value), grad_query)

    zero_state = jnp.zeros(key_row.shape, jnp.float32)
    block_shape = (block_count, block_len) + query_row.shape[1:]
    (grad_key, grad_value), grad_query = lax.scan(
        backward_one_block,
        (zero_state, zero_state),
        (
            query_row.reshape(block_shape),
            picture_row.reshape(block_count, block_len),
            grad_row.reshape(block_shape),
            logsum_row,
        ),
    )
    return (grad_query.reshape(key_row.shape), grad_key, grad_value)


def local(
    tokens,
    lengths,
    pictures,
    w_query,
    w_key,
    w_value,
    w_out,
    w_up,
    w_down,
    norm1_gain,
    norm1_shift,
    norm2_gain,
    norm2_shift,
    query_gain,
    key_gain,
    cotangent,
):
    tp_place = lax.axis_index("tp")
    local_len = tokens.shape[1]
    model_width = tokens.shape[2]
    full_len = pictures.shape[1]
    local_width = w_query.shape[1]
    heads_local = local_width // HD
    gain_one, shift_one, gain_two, shift_two, gain_query, gain_key = (
        lax.all_gather(norm1_gain, ("fsdp", "tp"), axis=0, tiled=True),
        lax.all_gather(norm1_shift, ("fsdp", "tp"), axis=0, tiled=True),
        lax.all_gather(norm2_gain, ("fsdp", "tp"), axis=0, tiled=True),
        lax.all_gather(norm2_shift, ("fsdp", "tp"), axis=0, tiled=True),
        lax.all_gather(query_gain, ("fsdp", "tp"), axis=0, tiled=True),
        lax.all_gather(key_gain, ("fsdp", "tp"), axis=0, tiled=True),
    )
    positions = jnp.arange(full_len, dtype=jnp.int32)
    valid_full = (positions[None, :] < jnp.sum(lengths, axis=1)[:, None]).astype(jnp.float32)
    valid_here = lax.dynamic_slice_in_dim(valid_full, tp_place * local_len, local_len, 1)[
        :, :, None
    ]
    qgain_here = lax.dynamic_slice_in_dim(
        gain_query, tp_place * local_width, local_width, 0
    ).reshape(heads_local, HD)
    kgain_here = lax.dynamic_slice_in_dim(gain_key, tp_place * local_width, local_width, 0).reshape(
        heads_local, HD
    )
    front_query, front_key, front_value, front_out = (
        lax.all_gather(w_query, "fsdp", axis=0, tiled=True),
        lax.all_gather(w_key, "fsdp", axis=0, tiled=True),
        lax.all_gather(w_value, "fsdp", axis=0, tiled=True),
        lax.all_gather(w_out, "fsdp", axis=1, tiled=True),
    )
    inputs = tokens.astype(jnp.float32)
    hidden, normed_one, inverse_one = normalise(inputs, gain_one, shift_one)
    hidden_full = gather_tokens(hidden.astype(jnp.bfloat16))
    row_shape = hidden_full.shape[:2] + (heads_local, HD)
    query = jnp.dot(hidden_full, front_query, preferred_element_type=jnp.float32).reshape(row_shape)
    keyed = jnp.dot(hidden_full, front_key, preferred_element_type=jnp.float32).reshape(row_shape)
    value_low = (
        jnp.dot(hidden_full, front_value, preferred_element_type=jnp.float32)
        .astype(jnp.bfloat16)
        .reshape(row_shape)
    )
    query_norm, query_unit, query_inverse = normalise(query, qgain_here, 0.0)
    key_norm, key_unit, key_inverse = normalise(keyed, kgain_here, 0.0)
    query_low = query_norm.astype(jnp.bfloat16)
    key_low = key_norm.astype(jnp.bfloat16)
    mixture, logsum = lax.map(forward_row, (query_low, key_low, value_low, pictures, valid_full))
    mixture_low = mixture.reshape(hidden_full.shape[:2] + (local_width,)).astype(jnp.bfloat16)
    attn_branch = valid_here * reduce_tokens(
        jnp.dot(mixture_low, front_out, preferred_element_type=jnp.float32)
    )
    middle = inputs + attn_branch
    hidden_two, normed_two, inverse_two = normalise(middle, gain_two, shift_two)
    hidden_two_full = gather_tokens(hidden_two.astype(jnp.bfloat16))
    front_up, front_down = (
        lax.all_gather(w_up, "fsdp", axis=0, tiled=True),
        lax.all_gather(w_down, "fsdp", axis=1, tiled=True),
    )
    up_value = jnp.dot(hidden_two_full, front_up, preferred_element_type=jnp.float32)
    activated = jax.nn.gelu(up_value, approximate=False).astype(jnp.bfloat16)
    mlp_branch = valid_here * reduce_tokens(
        jnp.dot(activated, front_down, preferred_element_type=jnp.float32)
    )
    result = (middle + mlp_branch).astype(jnp.bfloat16)
    square_sums = jnp.stack(
        [
            jnp.sum(valid_here * inputs * inputs),
            jnp.sum(attn_branch * attn_branch),
            jnp.sum(valid_here * middle * middle),
            jnp.sum(mlp_branch * mlp_branch),
        ]
    )
    valid_count = jnp.sum(valid_here)
    back_up, back_down = (
        lax.all_gather(w_up, "fsdp", axis=0, tiled=True),
        lax.all_gather(w_down, "fsdp", axis=1, tiled=True),
    )
    back_query, back_key, back_value, back_out = (
        lax.all_gather(w_query, "fsdp", axis=0, tiled=True),
        lax.all_gather(w_key, "fsdp", axis=0, tiled=True),
        lax.all_gather(w_value, "fsdp", axis=0, tiled=True),
        lax.all_gather(w_out, "fsdp", axis=1, tiled=True),
    )
    grad_y = cotangent.astype(jnp.float32) * valid_here
    grad_y_full = gather_grads(grad_y.astype(jnp.bfloat16))
    grad_down = jnp.einsum(
        "rlf,rld->fd", activated, grad_y_full, preferred_element_type=jnp.float32
    )
    grad_act = jnp.dot(grad_y_full, back_down.T, preferred_element_type=jnp.float32)
    grad_pre = (grad_act * gelu_slope(up_value)).astype(jnp.bfloat16)
    grad_up = jnp.einsum(
        "rld,rlf->df", hidden_two_full, grad_pre, preferred_element_type=jnp.float32
    )
    grad_hidden_two = reduce_grads(jnp.dot(grad_pre, back_up.T, preferred_element_type=jnp.float32))
    mlp_grads = (
        lax.psum_scatter(grad_up, "fsdp", scatter_dimension=0, tiled=True),
        lax.psum_scatter(grad_down, "fsdp", scatter_dimension=1, tiled=True),
    )
    grad_mid_norm, grad_gain_two, grad_shift_two = normalise_back(
        grad_hidden_two, normed_two, inverse_two, gain_two
    )
    grad_middle = grad_y + grad_mid_norm
    grad_branch_here = (valid_here * grad_middle).astype(jnp.bfloat16)
    grad_branch_full = gather_grads(grad_branch_here)
    grad_out_proj = jnp.einsum(
        "rlh,rld->hd", mixture_low, grad_branch_full, preferred_element_type=jnp.float32
    )
    grad_mixture = jnp.dot(grad_branch_full, back_out.T, preferred_element_type=jnp.float32).astype(
        jnp.bfloat16
    )
    grad_qnorm, grad_knorm, grad_value_full = lax.map(
        backward_row,
        (
            query_low,
            key_low,
            value_low,
            pictures,
            valid_full,
            grad_mixture.reshape(row_shape),
            logsum,
        ),
    )
    grad_query_pre, grad_qgain, unused_one = normalise_back(
        grad_qnorm, query_unit, query_inverse, qgain_here
    )
    grad_key_pre, grad_kgain, unused_two = normalise_back(
        grad_knorm, key_unit, key_inverse, kgain_here
    )
    flat_shape = hidden_full.shape[:2] + (local_width,)
    grad_query_low = grad_query_pre.reshape(flat_shape).astype(jnp.bfloat16)
    grad_key_low = grad_key_pre.reshape(flat_shape).astype(jnp.bfloat16)
    grad_value_low = grad_value_full.reshape(flat_shape).astype(jnp.bfloat16)
    grad_wquery = jnp.einsum(
        "rld,rlh->dh", hidden_full, grad_query_low, preferred_element_type=jnp.float32
    )
    grad_wkey = jnp.einsum(
        "rld,rlh->dh", hidden_full, grad_key_low, preferred_element_type=jnp.float32
    )
    grad_wvalue = jnp.einsum(
        "rld,rlh->dh", hidden_full, grad_value_low, preferred_element_type=jnp.float32
    )
    grad_hidden_part = (
        jnp.dot(grad_query_low, back_query.T, preferred_element_type=jnp.float32)
        + jnp.dot(grad_key_low, back_key.T, preferred_element_type=jnp.float32)
        + jnp.dot(grad_value_low, back_value.T, preferred_element_type=jnp.float32)
    )
    grad_hidden = reduce_grads(grad_hidden_part)
    attn_grads = (
        lax.psum_scatter(grad_wquery, "fsdp", scatter_dimension=0, tiled=True),
        lax.psum_scatter(grad_wkey, "fsdp", scatter_dimension=0, tiled=True),
        lax.psum_scatter(grad_wvalue, "fsdp", scatter_dimension=0, tiled=True),
        lax.psum_scatter(grad_out_proj, "fsdp", scatter_dimension=1, tiled=True),
    )
    grad_in_norm, grad_gain_one, grad_shift_one = normalise_back(
        grad_hidden, normed_one, inverse_one, gain_one
    )
    grad_inputs = grad_middle + grad_in_norm
    zero_width = jnp.zeros((model_width,), jnp.float32)
    grad_qgain_full = lax.dynamic_update_slice_in_dim(
        zero_width, grad_qgain.reshape(local_width), tp_place * local_width, 0
    )
    grad_kgain_full = lax.dynamic_update_slice_in_dim(
        zero_width, grad_kgain.reshape(local_width), tp_place * local_width, 0
    )
    small_shards = (
        lax.psum_scatter(grad_gain_one, ("fsdp", "tp"), scatter_dimension=0, tiled=True),
        lax.psum_scatter(grad_shift_one, ("fsdp", "tp"), scatter_dimension=0, tiled=True),
        lax.psum_scatter(grad_gain_two, ("fsdp", "tp"), scatter_dimension=0, tiled=True),
        lax.psum_scatter(grad_shift_two, ("fsdp", "tp"), scatter_dimension=0, tiled=True),
        lax.psum_scatter(grad_qgain_full, ("fsdp", "tp"), scatter_dimension=0, tiled=True),
        lax.psum_scatter(grad_kgain_full, ("fsdp", "tp"), scatter_dimension=0, tiled=True),
    )
    totals, counted = lax.psum((square_sums, valid_count), ("fsdp", "tp"))
    statistics = jnp.sqrt(totals / (counted * model_width))
    return (
        result,
        grad_inputs,
        attn_grads[0],
        attn_grads[1],
        attn_grads[2],
        attn_grads[3],
        mlp_grads[0],
        mlp_grads[1],
        small_shards[0],
        small_shards[1],
        small_shards[2],
        small_shards[3],
        small_shards[4],
        small_shards[5],
        statistics,
    )


def solution(mesh):
    in_specs = (
        P("fsdp", "tp", None),
        P("fsdp", None),
        P("fsdp", None),
        P("fsdp", "tp"),
        P("fsdp", "tp"),
        P("fsdp", "tp"),
        P("tp", "fsdp"),
        P("fsdp", "tp"),
        P("tp", "fsdp"),
        P(("fsdp", "tp")),
        P(("fsdp", "tp")),
        P(("fsdp", "tp")),
        P(("fsdp", "tp")),
        P(("fsdp", "tp")),
        P(("fsdp", "tp")),
        P("fsdp", "tp", None),
    )
    out_specs = (
        P("fsdp", "tp", None),
        P("fsdp", "tp", None),
        P("fsdp", "tp"),
        P("fsdp", "tp"),
        P("fsdp", "tp"),
        P("tp", "fsdp"),
        P("fsdp", "tp"),
        P("tp", "fsdp"),
        P(("fsdp", "tp")),
        P(("fsdp", "tp")),
        P(("fsdp", "tp")),
        P(("fsdp", "tp")),
        P(("fsdp", "tp")),
        P(("fsdp", "tp")),
        P(),
    )
    return jax.shard_map(local, mesh=mesh, in_specs=in_specs, out_specs=out_specs, check_vma=False)
```

profile of v0, /device:TPU:0, one launch (start us, length us, event | category | flops | bytes accessed | tf_op | source)
XLA Modules:
  0.0 1174.1 jit_solution(14461486698308457316)
XLA Ops:
  16.0 42.4 %all-reduce.13 = (f32[768]{0:T(1024)}, f32[768]{0:T(1024)}, f32[768]{0:T(1024)S(1)}, f32[768]{0:T(1024)S(1)}, f32[768]{0:T(1024)S(1)}, /*index=5*/f32[768]{0:T(1024)S(1)}) all-reduce(f32[768]{0:T(1024)S(1)} %dynamic-update-slice.5, f32[768]{0:T(1024)S(1)} %dynamic-update-slice.4, ...), channel_id=1, replica_groups=mesh['fsdp'=8,'tp'=4] {'fsdp','tp'}, use_global_device_ids=true, to_apply=%add.5 | all-reduce | flops 4608 | bytes 36864
  63.4 31.0 %all_gather.62 = bf16[192,768]{0,1:T(8,128)(2,1)S(1)} all-gather(bf16[192,96]{0,1:T(8,128)(2,1)S(1)} %copy.45), channel_id=1, replica_groups=mesh['fsdp'=8,'tp'=4] {'fsdp'}, dimensions={1}, use_global_device_ids=true | all-gather | bytes 331776 | tf_op jit(solution)/shard_map/all_gather | solution.py:178
  94.4 31.2 %all_gather.57 = bf16[768,192]{1,0:T(8,128)(2,1)S(1)} all-gather(bf16[96,192]{1,0:T(8,128)(2,1)S(1)} %copy-done.54), channel_id=1, replica_groups=mesh['fsdp'=8,'tp'=4] {'fsdp'}, dimensions={0}, use_global_device_ids=true | all-gather | bytes 331776 | tf_op jit(solution)/shard_map/all_gather | solution.py:175
  125.7 31.1 %all_gather.59 = bf16[768,192]{1,0:T(8,128)(2,1)S(1)} all-gather(bf16[96,192]{1,0:T(8,128)(2,1)S(1)} %copy-done.55), channel_id=1, replica_groups=mesh['fsdp'=8,'tp'=4] {'fsdp'}, dimensions={0}, use_global_device_ids=true | all-gather | bytes 331776 | tf_op jit(solution)/shard_map/all_gather | solution.py:176
  156.8 33.0 %all_gather.61 = bf16[768,192]{1,0:T(8,128)(2,1)} all-gather(bf16[96,192]{1,0:T(8,128)(2,1)S(1)} %copy-done.56), channel_id=1, replica_groups=mesh['fsdp'=8,'tp'=4] {'fsdp'}, dimensions={0}, use_global_device_ids=true | all-gather | bytes 331776 | tf_op jit(solution)/shard_map/all_gather | solution.py:177
  190.7 3.1 fusion.82
  196.5 3.1 fusion.80
  200.6 3.5 multiply_convert_fusion.4
  205.3 92.3 %while.50 = (s32[]{:T(128)}, bf16[4,512,3,64]{1,3,2,0:T(8,128)(2,1)}, f32[4,3,512,1]{2,1,3,0:T(4,128)}, s32[4,512]{1,0:T(4,128)S(1)}, s32[2048]{0:T(1024)S(1)}, ...) while((s32[]{:T(128)}, ...), condition=%wide.region_10.11_spmd.clone.clone, body=%wide.region_7.10_spmd.clone.sunk.clone | while | flops 842011136 | bytes 50469040 | solution.py:84
  206.9 6.8 fusion.199
  213.8 6.8 exponential_reduce_fusion.3
  221.2 6.4 fusion.200
  229.9 6.8 fusion.199
  236.8 6.8 exponential_reduce_fusion.3
  244.2 6.4 fusion.200
  253.0 6.8 fusion.199
  259.8 6.8 exponential_reduce_fusion.3
  267.2 6.4 fusion.200
  276.0 6.8 fusion.199
  282.8 6.8 exponential_reduce_fusion.3
  290.2 6.4 fusion.200
  304.1 36.6 %reduce-scatter.13.cloned.1.call-done = bf16[1,512,768]{2,1,0:T(8,128)(2,1)} async-done(((bf16[1,2048,768]{2,1,0:T(8,128)(2,1)}), bf16[1,512,768]{2,1,0:T(8,128)(2,1)}) %reduce-scatter.13.cloned.1.call-update) | async-done | bytes 786448 | tf_op jit(solution)/shard_map/reduce_scatter | solution.py:49
  342.4 4.1 fusion.117
  349.9 27.1 %all-gather.9.cloned.1.call-done = bf16[1,2048,768]{2,1,0:T(8,128)(2,1)} async-done(((bf16[1,512,768]{2,1,0:T(8,128)(2,1)}), bf16[1,2048,768]{2,1,0:T(8,128)(2,1)}) %all-gather.9.cloned.1.call-update) | async-done | bytes 3145744 | tf_op jit(solution)/shard_map/all_gather | solution.py:41
  377.0 18.6 %fusion.47 = (bf16[2048,768]{1,0:T(8,128)(2,1)}, f32[2048,768]{1,0:T(8,128)}) fusion(bf16[768,768]{1,0:T(8,128)(2,1)} %all-gather.11.cloned.1.call-done, bf16[1,2048,768]{2,1,0:T(8,128)(2,1)} %all-gather.9.cloned.1.call-done), kind=kOutput, calls=%fused_computation.61 | convolution fusion | flops 2518155264 | bytes 13762560 | tf_op jit(solution)/shard_map/dot_general | solution.py:207
  395.6 25.2 %all-gather.13.cloned.1.call-done = bf16[768,768]{0,1:T(8,128)(2,1)} async-done(((bf16[768,96]{0,1:T(8,128)(2,1)}), bf16[768,768]{0,1:T(8,128)(2,1)}) %all-gather.13.cloned.1.call-update) | async-done | bytes 1179664 | tf_op jit(solution)/shard_map/all_gather | solution.py:205
  420.9 29.1 %all-gather.15.cloned.1.call-done = bf16[1,2048,768]{2,1,0:T(8,128)(2,1)} async-done(((bf16[1,512,768]{2,1,0:T(8,128)(2,1)}), bf16[1,2048,768]{2,1,0:T(8,128)(2,1)}) %all-gather.15.cloned.1.call-update) | async-done | bytes 3145744 | tf_op jit(solution)/shard_map/all_gather | solution.py:45
  450.0 6.7 fusion.53
  458.3 4.0 fusion.86
  462.4 6.6 fusion.85
  469.0 31.4 %reduce-scatter.17.cloned.1.call-done = bf16[1,512,768]{2,1,0:T(8,128)(2,1)} async-done(((bf16[1,2048,768]{2,1,0:T(8,128)(2,1)}), bf16[1,512,768]{2,1,0:T(8,128)(2,1)}) %reduce-scatter.17.cloned.1.call-update) | async-done | bytes 786448 | tf_op jit(solution)/shard_map/reduce_scatter | solution.py:55
  500.5 40.4 %reduce-scatter.15.cloned.1.call-done = bf16[1,512,768]{2,1,0:T(8,128)(2,1)} async-done(((bf16[1,2048,768]{2,1,0:T(8,128)(2,1)}), bf16[1,512,768]{2,1,0:T(8,128)(2,1)}) %reduce-scatter.15.cloned.1.call-update) | async-done | bytes 786448 | tf_op jit(solution)/shard_map/reduce_scatter | solution.py:49
  540.9 4.2 fusion.115
  547.6 28.4 %all-gather.17.cloned.1.call-done = bf16[1,2048,768]{2,1,0:T(8,128)(2,1)} async-done(((bf16[1,512,768]{2,1,0:T(8,128)(2,1)}), bf16[1,2048,768]{2,1,0:T(8,128)(2,1)}) %all-gather.17.cloned.1.call-update) | async-done | bytes 3145744 | tf_op jit(solution)/shard_map/all_gather | solution.py:45
  576.0 3.1 fusion.91
  579.9 132.6 %while.51 = (s32[]{:T(128)}, f32[2048,3,64]{0,2,1:T(8,128)}, f32[2048,3,64]{0,2,1:T(8,128)}, f32[4,512,3,64]{1,3,2,0:T(8,128)}, bf16[4,512,3,64]{1,3,2,0:T(8,128...) while((s32[]{:T(128)}, f32[2048,3,64]{0,2,1:T(8,128)}, ...), condition=%wide.region_20.21_spmd.clone.clone, body=%wide.region_18.20_spmd.clone.sunk.clone | while | flops 2064617984 | bytes 169277904 | solution.py:118
  585.3 4.7 fusion.212
  590.1 5.8 multiply_reduce_fusion.14
  595.8 4.9 multiply_convert_fusion.7
  605.9 6.2 fusion.213
  617.3 6.1 fusion.212
  623.5 5.8 multiply_reduce_fusion.14
  629.2 4.9 multiply_convert_fusion.7
  639.3 6.2 fusion.213
  650.8 6.1 fusion.212
  656.9 5.8 multiply_reduce_fusion.14
  662.7 4.9 multiply_convert_fusion.7
  672.7 6.1 fusion.213
  684.2 6.1 fusion.212
  690.3 5.8 multiply_reduce_fusion.14
  696.1 4.9 multiply_convert_fusion.7
  706.1 6.2 fusion.213
  712.6 3.1 multiply_reduce_fusion.4
  731.9 6.0 fusion.68
  738.3 7.1 fusion.65
  756.3 4.2 fusion.76
  760.5 23.0 %reduce-scatter.31.cloned.1.call-done = f32[96,192]{1,0:T(8,128)} async-done(((f32[768,192]{1,0:T(8,128)}), f32[96,192]{1,0:T(8,128)}) %reduce-scatter.31.cloned.1.call-update) | async-done | bytes 73744
  785.1 37.7 %reduce-scatter.19.cloned.1.call-done = bf16[1,512,768]{2,1,0:T(8,128)(2,1)} async-done(((bf16[1,2048,768]{2,1,0:T(8,128)(2,1)}), bf16[1,512,768]{2,1,0:T(8,128)(2,1)}) %reduce-scatter.19.cloned.1.call-update) | async-done | bytes 786448 | tf_op jit(solution)/shard_map/reduce_scatter | solution.py:55
  824.8 41.4 %all-reduce.12 = (f32[768]{0:T(1024)S(1)}, f32[768]{0:T(1024)S(1)}, f32[768]{0:T(1024)S(1)}, f32[768]{0:T(1024)S(1)}, f32[768]{0:T(1024)S(1)}, /*index=5*/f32[768]{0:T(1024)S(1)}, f32[4]{0:T(128)S(1)}, f32[]{:T(128)}) all-reduce(f32[768]{0:T(1024)S(1)} %get-tuple-element.306, ...), channel_id=12, replica_groups=mesh['fsdp'=8,'tp'=4] {'fsdp','tp'}, use_global_device_ids=true, to_apply=%region_35.36.clone | all-reduce | flops 4613 | bytes 36904
  873.7 23.4 %reduce-scatter.27.cloned.1.call-done = f32[96,768]{1,0:T(8,128)} async-done(((f32[768,768]{1,0:T(8,128)}), f32[96,768]{1,0:T(8,128)}) %reduce-scatter.27.cloned.1.call-update) | async-done | bytes 294928 | tf_op jit(solution)/shard_map/reduce_scatter | solution.py:244
  897.1 72.5 %reduce-scatter.29.cloned.1.call-done = f32[768,96]{0,1:T(8,128)} async-done(((f32[768,768]{0,1:T(8,128)}), f32[768,96]{0,1:T(8,128)}) %reduce-scatter.29.cloned.1.call-update) | async-done | bytes 294928 | tf_op jit(solution)/shard_map/reduce_scatter | solution.py:245
  969.5 65.8 %reduce-scatter.23.cloned.1.call-done = f32[96,192]{1,0:T(8,128)} async-done(((f32[768,192]{1,0:T(8,128)}), f32[96,192]{1,0:T(8,128)}) %reduce-scatter.23.cloned.1.call-update) | async-done | bytes 73744 | tf_op jit(solution)/shard_map/reduce_scatter | solution.py:298
  1035.4 65.4 %reduce-scatter.25.cloned.1.call-done = f32[96,192]{1,0:T(8,128)} async-done(((f32[768,192]{1,0:T(8,128)}), f32[96,192]{1,0:T(8,128)}) %reduce-scatter.25.cloned.1.call-update) | async-done | bytes 73744 | tf_op jit(solution)/shard_map/reduce_scatter | solution.py:299
  1100.7 65.8 %reduce-scatter.21.cloned.1.call-done = f32[96,192]{1,0:T(8,128)} async-done(((f32[768,192]{1,0:T(8,128)}), f32[96,192]{1,0:T(8,128)}) %reduce-scatter.21.cloned.1.call-update) | async-done | bytes 73744 | tf_op jit(solution)/shard_map/reduce_scatter | solution.py:297
  (394 shorter events, 125.2 us)
Async XLA Ops:
  8.0 52.8 %copy-start.77 = (s32[1,4]{1,0:T(1,128)S(1)}, s32[1,4]{1,0:T(1,128)}, u32[]{:S(2)}) copy-start(s32[1,4]{1,0:T(1,128)} %param.21) | copy-start | bytes 52
  8.0 54.6 %copy-start.39 = (s32[1,2048]{1,0:T(1,128)S(1)}, s32[1,2048]{1,0:T(1,128)}, u32[]{:S(2)}) copy-start(s32[1,2048]{1,0:T(1,128)} %param.22) | copy-start | bytes 24580
  8.0 55.2 %copy-start.57 = (bf16[192,96]{1,0:T(8,128)(2,1)S(1)}, bf16[192,96]{1,0:T(8,128)(2,1)}, u32[]{:S(2)}) copy-start(bf16[192,96]{1,0:T(8,128)(2,1)} %param.26) | copy-start | bytes 110596
  8.0 86.4 %copy-start.54 = (bf16[96,192]{1,0:T(8,128)(2,1)S(1)}, bf16[96,192]{1,0:T(8,128)(2,1)}, u32[]{:S(2)}) copy-start(bf16[96,192]{1,0:T(8,128)(2,1)} %param.23) | copy-start | bytes 110596
  8.1 117.6 %copy-start.55 = (bf16[96,192]{1,0:T(8,128)(2,1)S(1)}, bf16[96,192]{1,0:T(8,128)(2,1)}, u32[]{:S(2)}) copy-start(bf16[96,192]{1,0:T(8,128)(2,1)} %param.24) | copy-start | bytes 110596
  8.1 148.7 %copy-start.56 = (bf16[96,192]{1,0:T(8,128)(2,1)S(1)}, bf16[96,192]{1,0:T(8,128)(2,1)}, u32[]{:S(2)}) copy-start(bf16[96,192]{1,0:T(8,128)(2,1)} %param.25) | copy-start | bytes 110596
  8.1 182.6 %all-gather.7.cloned.1.call-start = ((), (), s32[]{:S(2)}) async-start(), calls=%async_computation.10 | async-start | bytes 3932160 | tf_op jit(solution)/shard_map/all_gather | solution.py:41
  9.5 53.8 %copy-start.50 = (f32[512]{0:T(512)}, f32[512]{0:T(512)S(1)}, u32[]{:S(2)}) copy-start(f32[512]{0:T(512)S(1)} %broadcast_multiply_fusion.11) | copy-start | bytes 6148
  11.0 182.8 %copy-start.64 = (f32[512]{0:T(512)}, f32[512]{0:T(512)S(1)}, u32[]{:S(2)}) copy-start(f32[512]{0:T(512)S(1)} %add_rsqrt_fusion.3) | copy-start | bytes 6148
  58.4 135.4 %copy-start.58 = (f32[768]{0:T(1024)}, f32[768]{0:T(1024)S(1)}, u32[]{:S(2)}) copy-start(f32[768]{0:T(1024)S(1)} %get-tuple-element.372) | copy-start | bytes 9220
  60.8 279.9 %reduce-scatter.13.cloned.1.call-start = ((), (), s32[]{:S(2)}) async-start(), calls=%async_computation.11 | async-start | bytes 3932160 | tf_op jit(solution)/shard_map/reduce_scatter | solution.py:49
  61.7 138.2 %copy-start.62 = (f32[3,64]{1,0:T(4,128)}, f32[3,64]{1,0:T(4,128)S(1)}, u32[]{:S(2)}) copy-start(f32[3,64]{1,0:T(4,128)S(1)} %mul.406) | copy-start | bytes 2308
  62.1 138.2 %copy-start.68 = (f32[3,64]{1,0:T(4,128)}, f32[3,64]{1,0:T(4,128)S(1)}, u32[]{:S(2)}) copy-start(f32[3,64]{1,0:T(4,128)S(1)} %mul.400) | copy-start | bytes 2308
  125.7 68.1 %copy-start.27 = (bf16[768,192]{1,0:T(8,128)(2,1)}, bf16[768,192]{1,0:T(8,128)(2,1)S(1)}, u32[]{:S(2)}) copy-start(bf16[768,192]{1,0:T(8,128)(2,1)S(1)} %all_gather.57) | copy-start | bytes 884740
  156.8 39.6 %copy-start.25 = (bf16[768,192]{1,0:T(8,128)(2,1)}, bf16[768,192]{1,0:T(8,128)(2,1)S(1)}, u32[]{:S(2)}) copy-start(bf16[768,192]{1,0:T(8,128)(2,1)S(1)} %all_gather.59) | copy-start | bytes 884740
  213.8 7.4 copy-start.32
  236.8 7.4 copy-start.32
  259.8 7.4 copy-start.32
  282.8 7.4 copy-start.32
  299.5 41.2 %copy-start.4 = (bf16[1,512,768]{2,1,0:T(8,128)(2,1)S(1)}, bf16[1,512,768]{2,1,0:T(8,128)(2,1)}, u32[]{:S(2)}) copy-start(bf16[1,512,768]{2,1,0:T(8,128)(2,1)} %param.20) | copy-start | bytes 2359300
  302.2 47.7 %all-gather.11.cloned.1.call-start = ((), (), s32[]{:S(2)}) async-start(), calls=%async_computation.13 | async-start | bytes 1327104 | tf_op jit(solution)/shard_map/all_gather | solution.py:204
  302.8 74.2 %all-gather.9.cloned.1.call-start = ((), (), s32[]{:S(2)}) async-start(), calls=%async_computation.12 | async-start | bytes 3932160 | tf_op jit(solution)/shard_map/all_gather | solution.py:41
  340.7 6.4 copy-start.17
  340.7 6.4 copy-start.48
  340.7 6.4 copy-start.60
  340.7 6.4 copy-start.74
  348.5 72.3 %all-gather.13.cloned.1.call-start = ((), (), s32[]{:S(2)}) async-start(), calls=%async_computation.14 | async-start | bytes 1327104 | tf_op jit(solution)/shard_map/all_gather | solution.py:205
  349.1 100.9 %all-gather.15.cloned.1.call-start = ((), (), s32[]{:S(2)}) async-start(), calls=%async_computation.16 | async-start | bytes 3932160 | tf_op jit(solution)/shard_map/all_gather | solution.py:45
  349.8 150.6 %reduce-scatter.17.cloned.1.call-start = ((), (), s32[]{:S(2)}) async-start(), calls=%async_computation.17 | async-start | bytes 3932160 | tf_op jit(solution)/shard_map/reduce_scatter | solution.py:55
  450.0 8.3 copy-start.76
  462.4 78.5 %reduce-scatter.15.cloned.1.call-start = ((), (), s32[]{:S(2)}) async-start(), calls=%async_computation.15 | async-start | bytes 3932160 | tf_op jit(solution)/shard_map/reduce_scatter | solution.py:49
  469.0 107.0 %all-gather.17.cloned.1.call-start = ((), (), s32[]{:S(2)}) async-start(), calls=%async_computation.18 | async-start | bytes 3932160 | tf_op jit(solution)/shard_map/all_gather | solution.py:45
  547.5 235.9 %reduce-scatter.31.cloned.1.call-start = ((), (), s32[]{:S(2)}) async-start(), calls=%async_computation.25 | async-start | bytes 884736
  579.8 132.7 %copy-start.41 = (f32[2048,3]{0,1:T(4,128)S(1)}, f32[2048,3]{0,1:T(4,128)}, u32[]{:S(2)}) copy-start(f32[2048,3]{0,1:T(4,128)} %copy-done.40) | copy-start | bytes 73732
  579.9 132.7 %copy-start.45 = (f32[2048,3]{0,1:T(4,128)S(1)}, f32[2048,3]{0,1:T(4,128)}, u32[]{:S(2)}) copy-start(f32[2048,3]{0,1:T(4,128)} %copy-done.44) | copy-start | bytes 73732
  579.9 132.7 %copy-start.69 = (f32[3,64]{1,0:T(4,128)S(1)}, f32[3,64]{1,0:T(4,128)}, u32[]{:S(2)}) copy-start(f32[3,64]{1,0:T(4,128)} %copy-done.68) | copy-start | bytes 2308
  595.8 7.6 copy-start.6
  605.8 6.2 copy-start.7
  605.9 6.2 copy-start.12
  605.9 6.2 copy-start.24
  629.2 7.6 copy-start.6
  639.2 6.2 copy-start.7
  639.3 6.2 copy-start.12
  639.3 6.2 copy-start.24
  662.7 7.6 copy-start.6
  672.7 6.2 copy-start.7
  696.0 7.6 copy-start.6
  706.1 6.2 copy-start.7
  706.1 6.2 copy-start.12
  706.1 6.2 copy-start.24
  720.8 101.9 %reduce-scatter.19.cloned.1.call-start = ((), (), s32[]{:S(2)}) async-start(), calls=%async_computation.19 | async-start | bytes 3932160 | tf_op jit(solution)/shard_map/reduce_scatter | solution.py:55
  730.0 167.0 %reduce-scatter.27.cloned.1.call-start = ((), (), s32[]{:S(2)}) async-start(), calls=%async_computation.23 | async-start | bytes 2654208 | tf_op jit(solution)/shard_map/reduce_scatter | solution.py:244
  738.0 7.5 copy-start.16
  738.0 231.6 %reduce-scatter.29.cloned.1.call-start = ((), (), s32[]{:S(2)}) async-start(), calls=%async_computation.24 | async-start | bytes 2654208 | tf_op jit(solution)/shard_map/reduce_scatter | solution.py:245
  745.4 289.9 %reduce-scatter.23.cloned.1.call-start = ((), (), s32[]{:S(2)}) async-start(), calls=%async_computation.21 | async-start | bytes 884736 | tf_op jit(solution)/shard_map/reduce_scatter | solution.py:298
  748.6 352.1 %reduce-scatter.25.cloned.1.call-start = ((), (), s32[]{:S(2)}) async-start(), calls=%async_computation.22 | async-start | bytes 884736 | tf_op jit(solution)/shard_map/reduce_scatter | solution.py:299
  751.7 414.8 %reduce-scatter.21.cloned.1.call-start = ((), (), s32[]{:S(2)}) async-start(), calls=%async_computation.20 | async-start | bytes 884736 | tf_op jit(solution)/shard_map/reduce_scatter | solution.py:297
  756.2 66.6 %copy-start.5 = (bf16[1,512,768]{2,1,0:T(8,128)(2,1)S(1)}, bf16[1,512,768]{2,1,0:T(8,128)(2,1)}, u32[]{:S(2)}) copy-start(bf16[1,512,768]{2,1,0:T(8,128)(2,1)} %param.20) | copy-start | bytes 2359300
  756.2 66.6 %copy-start.51 = (f32[512]{0:T(512)S(1)}, f32[512]{0:T(512)}, u32[]{:S(2)}) copy-start(f32[512]{0:T(512)} %copy-done.50) | copy-start | bytes 6148
  756.2 66.6 %copy-start.59 = (f32[768]{0:T(1024)S(1)}, f32[768]{0:T(1024)}, u32[]{:S(2)}) copy-start(f32[768]{0:T(1024)} %copy-done.58) | copy-start | bytes 9220
  756.2 66.6 %copy-start.65 = (f32[512]{0:T(512)S(1)}, f32[512]{0:T(512)}, u32[]{:S(2)}) copy-start(f32[512]{0:T(512)} %copy-done.64) | copy-start | bytes 6148
  756.2 68.5 %copy-start.70 = (f32[768]{0:T(1024)S(1)}, f32[768]{0:T(1024)}, u32[]{:S(2)}) copy-start(f32[768]{0:T(1024)} %get-tuple-element.304) | copy-start | bytes 9220
  756.3 68.5 %copy-start.71 = (f32[768]{0:T(1024)S(1)}, f32[768]{0:T(1024)}, u32[]{:S(2)}) copy-start(f32[768]{0:T(1024)} %get-tuple-element.316) | copy-start | bytes 9220
  756.3 114.5 %copy-start.20 = (f32[1,512,768]{2,1,0:T(8,128)S(1)}, f32[1,512,768]{2,1,0:T(8,128)}, u32[]{:S(2)}) copy-start(f32[1,512,768]{2,1,0:T(8,128)} %get-tuple-element.378) | copy-start | bytes 4718596
  (67 other events, 210.4 us)
Sparse Core Ops, SparseCore 0:
  60.9 28.6 all-gather.6
  302.3 38.2 reduce-scatter.12
  462.5 37.9 reduce-scatter.16
  502.9 37.9 reduce-scatter.14
Sparse Core Ops, SparseCore 1:
  305.1 41.8 all-gather.10
  348.6 28.3 all-gather.8
  379.3 41.5 all-gather.12
  423.1 26.8 all-gather.14
  547.6 28.3 all-gather.16
  720.9 62.5 reduce-scatter.30
  785.9 36.9 reduce-scatter.18
  827.1 69.9 reduce-scatter.26
  901.4 68.1 reduce-scatter.28
  973.8 61.5 reduce-scatter.22
  1039.1 61.6 reduce-scatter.24
  1105.0 61.5 reduce-scatter.20
where the time goes:
time: 1180 us; the launch traced here: 1170 us
  waiting for transfers between devices  574 us (49%)
  matrix products  225 us (19%)
  blocking collectives  210 us (18%)
  other arithmetic  103 us (9%)
  local copies, waits for them, and re-layouts  42 us (4%)
  between operations  17.5 us (1%)
    unnamed x2, blocking collectives  83.7 us
    reduce_scatter x2, waiting for transfers between devices, reduce_tokens(): lax.psum_scatter(values.astype(jnp.bfloat16), 'tp', scatter_dimension=1,...  77 us
    reduce_scatter x1, waiting for transfers between devices, local(): lax.psum_scatter(grad_down, 'fsdp', scatter_dimension=1, tiled=True)  72.5 us
    reduce_scatter x2, waiting for transfers between devices, reduce_grads(): lax.psum_scatter(values.astype(jnp.bfloat16), 'tp', scatter_dimension=1,...  69.1 us
    reduce_scatter x1, waiting for transfers between devices, local(): lax.psum_scatter(grad_wkey, 'fsdp', scatter_dimension=0, tiled=True)  65.8 us
    reduce_scatter x1, waiting for transfers between devices, local(): lax.psum_scatter(grad_wquery, 'fsdp', scatter_dimension=0, tiled=True)  65.8 us
    reduce_scatter x1, waiting for transfers between devices, local(): lax.psum_scatter(grad_wvalue, 'fsdp', scatter_dimension=0, tiled=True)  65.4 us
    all_gather x2, waiting for transfers between devices, gather_grads(): return lax.all_gather(values, 'tp', axis=1, tiled=True)  57.5 us
  transfers between devices with their start and end apart: 16, of which 14 were waited for; matrix products, arithmetic and copies ran while one was open for 7% of the time, Pallas kernels for 0%

commit v1 on v0

--- a/solution.py
+++ b/solution.py
@@ -1,9 +1,532 @@
+import functools
+
 import jax
 import jax.numpy as jnp
 from jax import lax
+from jax.experimental import pallas as pl
+from jax.experimental.pallas import tpu as pltpu
 from jax.sharding import PartitionSpec as P
 
 HD = 64
+BIG = 1024
+SMALL = 448
+LP = BIG + 3 * SMALL
+MARGIN = 128
+EXP_SCALE = 0.125 * 1.4426950408889634
+MESH = pl.DeviceIdType.MESH
+BF = jnp.bfloat16
+F32 = jnp.float32
+
+
+def dot_nn(a, b):
+    return lax.dot_general(a, b, (((1,), (0,)), ((), ())), preferred_element_type=F32)
+
+
+def dot_nt(a, b):
+    return lax.dot_general(a, b, (((1,), (1,)), ((), ())), preferred_element_type=F32)
+
+
+def dot_tn(a, b):
+    return lax.dot_general(a, b, (((0,), (0,)), ((), ())), preferred_element_type=F32)
+
+
+def iota(shape, dim):
+    return lax.broadcasted_iota(jnp.int32, shape, dim)
+
+
+def head_mask(rows, width, h):
+    lane = iota((rows, width), 1)
+    return (lane >= h * HD) & (lane < (h + 1) * HD)
+
+
+def segment_matrix(width):
+    r = iota((width, width), 0) // HD
+    c = iota((width, width), 1) // HD
+    return jnp.where(r == c, 1.0 / HD, 0.0).astype(BF)
+
+
+def segment_mean(x, seg):
+    hi = x.astype(BF)
+    lo = (x - hi.astype(F32)).astype(BF)
+    return dot_nn(hi, seg) + dot_nn(lo, seg)
+
+
+class Place:
+    def __init__(self, nf, nt):
+        self.nf, self.nt = nf, nt
+        self.nx = 2
+        self.nz = nf // 2
+        f = lax.axis_index("fsdp")
+        t = lax.axis_index("tp")
+        self.f, self.t = f, t
+        self.z, self.x = f // 2, lax.rem(f, 2)
+        self.y, self.c = t // 2, lax.rem(t, 2)
+        self.me = f * nt + t
+
+    def rel(self, dz=0, dx=0, dy=0, dc=0):
+        z = lax.rem(self.z + dz, self.nz) if dz else self.z
+        x = 1 - self.x if dx else self.x
+        y = 1 - self.y if dy else self.y
+        c = 1 - self.c if dc else self.c
+        return (z * 2 + x, y * 2 + c)
+
+
+class Copies:
+    def __init__(self):
+        self.sent = []
+
+    def start(self, src, dst, send_sem, recv_sem, dev):
+        cp = pltpu.make_async_remote_copy(
+            src_ref=src,
+            dst_ref=dst,
+            send_sem=send_sem,
+            recv_sem=recv_sem,
+            device_id=dev,
+            device_id_type=MESH,
+        )
+        cp.start()
+        self.sent.append(cp)
+
+    def finish(self):
+        for cp in self.sent:
+            cp.wait_send()
+        self.sent = []
+
+
+def wait_recv(dst, send_sem, recv_sem, dev):
+    pltpu.make_async_remote_copy(
+        src_ref=dst,
+        dst_ref=dst,
+        send_sem=send_sem,
+        recv_sem=recv_sem,
+        device_id=dev,
+        device_id_type=MESH,
+    ).wait_recv()
+
+
+def barrier_all(pc):
+    n = pc.nf * pc.nt
+    bar = pltpu.get_barrier_semaphore()
+
+    def body(r, carry):
+        p = lax.rem(pc.me + r, n)
+        pl.semaphore_signal(
+            bar, inc=1, device_id=(p // pc.nt, lax.rem(p, pc.nt)), device_id_type=MESH
+        )
+        return carry
+
+    lax.fori_loop(1, n, body, 0)
+    pl.semaphore_wait(bar, n - 1)
+
+
+GATHER_ORDERS = {"zxy": ("z", "x", "y"), "zyx": ("z", "y", "x")}
+
+
+def axis_steps(pc, axis):
+    if axis == "z":
+        return [dict(dz=i) for i in range(1, pc.nz)]
+    return [{"d" + axis: 1}]
+
+
+def gather_plan(pc, order):
+    stages = [[(dict(), 0)]]
+    have = [dict()]
+    for k, axis in enumerate(order):
+        fresh = []
+        for step in axis_steps(pc, axis):
+            for b in have:
+                fresh.append(dict(b, **step))
+        stages.append([(b, k + 1) for b in fresh])
+        have = have + fresh
+    return stages
+
+
+class Gather:
+    def __init__(self, pc, copies, src, dst, send, recv, order, spread_tp=True):
+        self.pc, self.copies = pc, copies
+        self.src, self.dst, self.send, self.recv = src, dst, send, recv
+        self.order = order
+        self.spread_tp = spread_tp
+        self.stages = gather_plan(pc, order)
+        self.count = 0
+
+    def slot(self, place):
+        f, t = place
+        return self.dst.at[t, f] if self.spread_tp else self.dst.at[f]
+
+    def rsem(self, place):
+        f, t = place
+        return self.recv.at[t, f] if self.spread_tp else self.recv.at[f]
+
+    def pass_on(self, block, depth):
+        pc = self.pc
+        place = pc.rel(**block)
+        src = self.src if not block else self.slot(place)
+        targets = []
+        for axis in self.order[depth:]:
+            targets += axis_steps(pc, axis)
+        if self.spread_tp:
+            targets.append(dict(dc=1))
+        for step in targets:
+            self.copies.start(
+                src,
+                self.slot(place),
+                self.send.at[self.count],
+                self.rsem(place),
+                pc.rel(**step),
+            )
+            self.count += 1
+
+    def wait(self, block):
+        place = self.pc.rel(**block)
+        wait_recv(self.slot(place), self.send.at[0], self.rsem(place), self.pc.rel(dc=1))
+
+    def stage(self, k):
+        for block, depth in self.stages[k]:
+            if block:
+                self.wait(block)
+            self.pass_on(block, depth)
+
+    def last(self):
+        if self.spread_tp:
+            for stage in self.stages:
+                for block, depth in stage:
+                    self.wait(dict(block, dc=1))
+
+
+def sends_of(nz, order, spread_tp):
+    n = {"z": nz - 1, "x": 1, "y": 1}
+    total, have = 0, 1
+    for axis in order:
+        total += have * n[axis]
+        have *= n[axis] + 1
+    return total + (have if spread_tp else 0)
+
+
+def slots_of(lens_ref):
+    lens = [lens_ref[0, p] for p in range(4)]
+    starts = [0]
+    for p in range(3):
+        starts.append(starts[-1] + lens[p])
+    big = 0
+    for p in range(1, 4):
+        big = jnp.where(lens[p] == BIG, p, big)
+    sb = 0
+    for p in range(1, 4):
+        sb = jnp.where(big == p, starts[p], sb)
+    out = [(sb, BIG)]
+    for k in range(3):
+        s = jnp.where(big <= k, starts[k + 1], starts[k])
+        n = jnp.where(big <= k, lens[k + 1], lens[k])
+        out.append((s, n))
+    return out
+
+
+BASES = (0, BIG, BIG + SMALL, BIG + 2 * SMALL)
+
+
+def shift_matrix(rows, cols, r):
+    return jnp.where(iota((rows, cols), 1) == iota((rows, cols), 0) + r, 1.0, 0.0).astype(BF)
+
+
+def load_rows(src, first, count):
+    return jnp.concatenate([src[first + m] for m in range(count)], axis=0)
+
+
+def pack_rows(src, dst, lens):
+    def big(j, carry):
+        s = slots_of(lens)[0][0]
+        r = lax.rem(s, 16)
+        d = shift_matrix(128, 144, r)
+        out = dot_nn(d, load_rows(src, s // 16 + j * 8, 9)).astype(BF)
+        dst[pl.ds(pl.multiple_of(j * 128, 128), 128), :] = out
+        return carry
+
+    lax.fori_loop(0, BIG // 128, big, 0)
+
+    for k in range(3):
+
+        def small(j, carry, k=k):
+            s = slots_of(lens)[1 + k][0]
+            r = lax.rem(s, 16)
+            d = shift_matrix(112, 128, r)
+            out = dot_nn(d, load_rows(src, s // 16 + j * 7, 8)).astype(BF)
+            dst[pl.ds(pl.multiple_of(BASES[1 + k] + j * 112, 16), 112), :] = out
+            return carry
+
+        lax.fori_loop(0, 4, small, 0)
+
+
+def unpack_tile(src, i0, lens):
+    wa, ea, wb, sb = 0, 0, 0, 4096
+    for (s, n), base in zip(slots_of(lens), BASES):
+        inside = (s <= i0) & (i0 < s + n)
+        begins = (s > i0) & (s <= i0 + 127)
+        w = base + i0 - s + MARGIN
+        wa = jnp.where(inside, w, wa)
+        ea = jnp.where(inside, s + n - i0, ea)
+        wb = jnp.where(begins, w, wb)
+        sb = jnp.where(begins, s - i0, sb)
+    out = None
+    row = iota((128, 144), 0)
+    col = iota((128, 144), 1)
+    for w, ok in ((wa, lambda: row < ea), (wb, lambda: row >= sb)):
+        r = lax.rem(w, 16)
+        d = jnp.where((col == row + r) & ok(), 1.0, 0.0).astype(BF)
+        part = dot_nn(d, load_rows(src, w // 16, 9))
+        out = part if out is None else out + part
+    return out
+
+
+def layer_norm_rows(x, g, b):
+    mean = jnp.mean(x, axis=-1, keepdims=True)
+    xc = x - mean
+    var = jnp.mean(xc * xc, axis=-1, keepdims=True)
+    inv = lax.rsqrt(var + EPS)
+    n = xc * inv
+    return n * g + b, n, inv
+
+
+def own_heads(row, t, nt, width):
+    out = row[:, :width]
+    for k in range(1, nt):
+        out = jnp.where(t == k, row[:, k * width : (k + 1) * width], out)
+    return out
+
+
+def build_gains(prm_all, gains, n, per):
+    chunks = n * per // 128
+    lane = iota((8, 128), 1)
+    acc = [jnp.zeros((8, 128), F32) for _ in range(chunks)]
+    for d in range(n):
+        j, a = divmod(d * per, 128)
+        tile = prm_all[d]
+        if a:
+            tile = pltpu.roll(tile, a, 1)
+        acc[j] = jnp.where((lane >= a) & (lane < a + per), tile, acc[j])
+        if a + per > 128:
+            acc[j + 1] = jnp.where(lane < a + per - 128, tile, acc[j + 1])
+    for j in range(chunks):
+        gains[:, j * 128 : (j + 1) * 128] = acc[j]
+
+
+def ka_kernel(
+    nf, nt, orders,
+    lens, tok, wa, wo, wu, wd, prm,
+    h1p, qraw, kraw, qn, kn, va, lse, of, wqkv, wo_all, wu_all, wd_all, gains, o_own,
+    tok_all, h1t, wa_all, prm_all, op, osend,
+    prm_s, prm_r, tok_s, tok_r, wa_s, wa_r, wo_s, wo_r, wu_s, wu_r, wd_s, wd_r, o_s, o_r, loc,
+):
+    pc = Place(nf, nt)
+    n = nf * nt
+    cps = Copies()
+    rows, width = tok.shape
+    hw = qn.shape[1]
+    barrier_all(pc)
+
+    cps.start(tok, tok_all.at[pc.t], tok_s.at[0], tok_r.at[pc.t], pc.rel(dy=1))
+    cps.start(tok, tok_all.at[pc.t], tok_s.at[1], tok_r.at[pc.t], pc.rel(dc=1))
+
+    def push_prm(r, carry):
+        p = lax.rem(pc.me + r, n)
+        pltpu.make_async_remote_copy(
+            src_ref=prm, dst_ref=prm_all.at[pc.me], send_sem=prm_s.at[r], recv_sem=prm_r.at[pc.me],
+            device_id=(p // nt, lax.rem(p, nt)), device_id_type=MESH,
+        ).start()
+        return carry
+
+    lax.fori_loop(1, n, push_prm, 0)
+    ga = Gather(pc, cps, wa, wa_all, wa_s, wa_r, ("z", "x"), False)
+    gw = [
+        Gather(pc, cps, wo, wo_all, wo_s, wo_r, orders[0]),
+        Gather(pc, cps, wu, wu_all, wu_s, wu_r, orders[1]),
+        Gather(pc, cps, wd, wd_all, wd_s, wd_r, orders[2]),
+    ]
+    ga.stage(0)
+    for g in gw:
+        g.stage(0)
+    local = []
+    for src, dst in ((tok, tok_all.at[pc.t]), (wa, wa_all.at[pc.f]), (wo, wo_all.at[pc.t, pc.f]),
+                     (wu, wu_all.at[pc.t, pc.f]), (wd, wd_all.at[pc.t, pc.f])):
+        cp = pltpu.make_async_copy(src, dst, loc.at[len(local)])
+        cp.start()
+        local.append(cp)
+    prm_all[pc.me] = prm[...]
+
+    h1t[4 * rows // 16 :] = jnp.zeros((h1t.shape[0] - 4 * rows // 16, 16, width), BF)
+
+    def wait_prm(r, carry):
+        p = lax.rem(pc.me + r, n)
+        wait_recv(prm_all.at[p], prm_s.at[0], prm_r.at[p], (p // nt, lax.rem(p, nt)))
+        return carry
+
+    lax.fori_loop(1, n, wait_prm, 0)
+    build_gains(prm_all, gains, n, width // n)
+    gain_one, shift_one = gains[0:1, :], gains[1:2, :]
+
+    def norm_block(t):
+        def body(j, carry):
+            at = pl.ds(pl.multiple_of(j * 128, 128), 128)
+            out, _, _ = layer_norm_rows(tok_all[t, at, :].astype(F32), gain_one, shift_one)
+            h1t[pl.ds(t * (rows // 16) + j * 8, 8)] = out.astype(BF).reshape(8, 16, width)
+            return carry
+
+        lax.fori_loop(0, rows // 128, body, 0)
+
+    def wait_tok(t):
+        wait_recv(tok_all.at[t], tok_s.at[0], tok_r.at[t], pc.rel(dc=1))
+
+    for cp in local:
+        cp.wait()
+    norm_block(pc.t)
+    t_core, t_y, t_diag = pc.rel(dc=1)[1], pc.rel(dy=1)[1], pc.rel(dy=1, dc=1)[1]
+    wait_tok(t_core)
+    norm_block(t_core)
+    ga.stage(1)
+    for g in gw:
+        g.stage(1)
+    wait_tok(t_y)
+    cps.start(tok_all.at[t_y], tok_all.at[t_y], tok_s.at[2], tok_r.at[t_y], pc.rel(dc=1))
+    norm_block(t_y)
+    ga.stage(2)
+    wait_tok(t_diag)
+    norm_block(t_diag)
+
+    pack_rows(h1t, h1p, lens)
+    seg = segment_matrix(hw)
+    gq = own_heads(gains[4:5, :], pc.t, nt, hw)
+    gk = own_heads(gains[5:6, :], pc.t, nt, hw)
+    w_full = wa_all[...].reshape(width, 3 * hw)
+    for i in range(3):
+        wqkv[i] = w_full[:, i * hw : (i + 1) * hw]
+
+    qt = LP // 4
+
+    def project(j, carry):
+        at = pl.ds(pl.multiple_of(j * qt, 16), qt)
+        h = h1p[at, :]
+        for i, (raw, normed, g) in enumerate(((qraw, qn, gq), (kraw, kn, gk))):
+            q = dot_nn(h, wqkv[i])
+            raw[at, :] = q
+            qc = q - segment_mean(q, seg)
+            inv = lax.rsqrt(segment_mean(qc * qc, seg) + EPS)
+            normed[at, :] = (qc * inv * g).astype(BF)
+        v = dot_nn(h, wqkv[2]).astype(BF)
+        va[at, :hw] = v
+        return carry
+
+    lax.fori_loop(0, 4, project, 0)
+    va[:, hw:] = jnp.ones((LP, va.shape[1] - hw), BF)
+    head, tail = MARGIN // 16, (MARGIN + LP) // 16
+    op[:head] = jnp.zeros((head, 16, hw), BF)
+    op[tail:] = jnp.zeros((op.shape[0] - tail, 16, hw), BF)
+
+    for g in gw:
+        g.stage(2)
+
+    def attend(at, keys, h, limit):
+        nrow = at.size
+        q = jnp.where(head_mask(nrow, hw, h), qn[at, :], jnp.zeros((), BF))
+        s = dot_nt(q, kn[keys, :])
+        p = jnp.exp2(s * EXP_SCALE)
+        if limit is not None:
+            p = jnp.where(iota(p.shape, 1) < limit, p, 0.0)
+        oa = dot_nn(p.astype(BF), va[keys, :])
+        total = oa[:, hw : hw + 1]
+        o = oa[:, :hw] * (1.0 / total)
+        l2 = jnp.log2(total)
+        lane = iota((nrow, 128), 1)
+        if h == 0:
+            of[at, :] = o
+            lse[at, :] = jnp.broadcast_to(l2, (nrow, 128))
+        else:
+            of[at, :] = jnp.where(head_mask(nrow, hw, h), o, of[at, :])
+            lse[at, :] = jnp.where(lane == h, l2, lse[at, :])
+
+    nh = hw // HD
+    for h in range(nh):
+        def big(j, carry, h=h):
+            attend(pl.ds(pl.multiple_of(j * 512, 512), 512), pl.ds(0, BIG), h, None)
+            return carry
+
+        lax.fori_loop(0, BIG // 512, big, 0)
+
+        for k in range(3):
+            at = pl.ds(BASES[1 + k], SMALL)
+            attend(at, at, h, slots_of(lens)[1 + k][1])
+        if h == 0:
+            for g in gw:
+                g.stage(3)
+
+    op[head:tail] = of[...].astype(BF).reshape(LP // 16, 16, hw)
+
+    def unpack(i, carry):
+        out = unpack_tile(op, i * 128, lens)
+        osend[i // 4, pl.ds(pl.multiple_of(lax.rem(i, 4) * 128, 128), 128), :] = out.astype(BF)
+        return carry
+
+    lax.fori_loop(0, 16, unpack, 0)
+    peers = [pc.rel(dy=1), pc.rel(dy=1, dc=1), pc.rel(dc=1)]
+    for i, dev in enumerate(peers):
+        cps.start(osend.at[dev[1]], o_own.at[pc.t], o_s.at[i], o_r.at[pc.t], dev)
+    cp = pltpu.make_async_copy(osend.at[pc.t], o_own.at[pc.t], loc.at[0])
+    cp.start()
+    cp.wait()
+    for g in gw:
+        g.last()
+    for dev in peers:
+        wait_recv(o_own.at[dev[1]], o_s.at[0], o_r.at[dev[1]], dev)
+
+    def wait_prm_sent(r, carry):
+        p = lax.rem(pc.me + r, n)
+        pltpu.make_async_remote_copy(
+            src_ref=prm, dst_ref=prm_all.at[pc.me], send_sem=prm_s.at[r], recv_sem=prm_r.at[pc.me],
+            device_id=(p // nt, lax.rem(p, nt)), device_id_type=MESH,
+        ).wait_send()
+        return carry
+
+    lax.fori_loop(1, n, wait_prm_sent, 0)
+    cps.finish()
+
+
+def call_ka(nf, nt, lens, tok, wa, wo, wu, wd, prm):
+    nz = nf // 2
+    rows, width = tok.shape
+    r = wa.shape[0]
+    hw = wa.shape[1] // 3
+    cu, cd = wu.shape[1], wd.shape[1]
+    orders = (("z", "x", "y"), ("z", "y", "x"), ("z", "x", "y"))
+    S = jax.ShapeDtypeStruct
+    vm = pl.BlockSpec(memory_space=pltpu.VMEM)
+    hb = pl.BlockSpec(memory_space=pl.ANY)
+    outs = [
+        (S((LP, width), BF), vm), (S((LP, hw), F32), vm), (S((LP, hw), F32), vm),
+        (S((LP, hw), BF), vm), (S((LP, hw), BF), vm), (S((LP, 256), BF), vm),
+        (S((LP, 128), F32), vm), (S((LP, hw), F32), vm), (S((3, width, hw), BF), vm),
+        (S((nt, nf, r, hw), BF), hb), (S((nt, nf, r, cu), BF), hb), (S((nt, nf, r, cd), BF), hb),
+        (S((8, width), F32), vm), (S((nt, rows, hw), BF), vm),
+    ]
+    dma = pltpu.SemaphoreType.DMA
+    sends = [sends_of(nz, o, True) for o in orders]
+    scratch = [
+        pltpu.VMEM((nt, rows, width), BF), pltpu.VMEM(((nt * rows + 192) // 16, 16, width), BF),
+        pltpu.VMEM((nf, r, 3 * hw), BF), pltpu.VMEM((nf * nt, 8, 128), F32),
+        pltpu.VMEM(((MARGIN + LP + 160) // 16, 16, hw), BF), pltpu.VMEM((nt, rows, hw), BF),
+        dma((nf * nt,)), dma((nf * nt,)), dma((3,)), dma((nt,)),
+        dma((sends_of(nz, ("z", "x"), False),)), dma((nf,)),
+        dma((sends[0],)), dma((nt, nf)), dma((sends[1],)), dma((nt, nf)), dma((sends[2],)), dma((nt, nf)),
+        dma((3,)), dma((nt,)), dma((5,)),
+    ]
+    return pl.pallas_call(
+        functools.partial(ka_kernel, nf, nt, orders),
+        out_shape=[o[0] for o in outs],
+        in_specs=[pl.BlockSpec(memory_space=pltpu.SMEM), vm, vm, hb, hb, hb, vm],
+        out_specs=[o[1] for o in outs],
+        scratch_shapes=scratch,
+        compiler_params=pltpu.CompilerParams(
+            collective_id=0, has_side_effects=True, vmem_limit_bytes=56 << 20
+        ),
+    )(lens, tok, wa, wo, wu, wd, prm)
 
 
 EPS = 1e-06
@@ -128,7 +651,9 @@
     return (grad_query.reshape(key_row.shape), grad_key, grad_value)
 
 
-def local(
+def local_layer(
+    nf,
+    nt,
     tokens,
     lengths,
     pictures,
@@ -177,6 +702,13 @@
         lax.all_gather(w_value, "fsdp", axis=0, tiled=True),
         lax.all_gather(w_out, "fsdp", axis=1, tiled=True),
     )
+    fused = nt == 4 and tokens.shape[0] == 1 and w_query.shape[0] % 16 == 0
+    if fused:
+        smalls = (norm1_gain, norm1_shift, norm2_gain, norm2_shift, query_gain, key_gain)
+        per = norm1_gain.shape[0]
+        prm = jnp.zeros((8, 128), jnp.float32).at[:6, :per].set(jnp.stack(smalls))
+        attn = jnp.concatenate([w_query, w_key, w_value], axis=1)
+        ka = call_ka(nf, nt, lengths, tokens[0], attn, w_out.T, w_up, w_down.T, prm)
     inputs = tokens.astype(jnp.float32)
     hidden, normed_one, inverse_one = normalise(inputs, gain_one, shift_one)
     hidden_full = gather_tokens(hidden.astype(jnp.bfloat16))
@@ -197,6 +729,10 @@
     attn_branch = valid_here * reduce_tokens(
         jnp.dot(mixture_low, front_out, preferred_element_type=jnp.float32)
     )
+    if fused:
+        mixed = jnp.transpose(ka[13], (1, 0, 2)).reshape(local_len, model_width)
+        w_full = jnp.transpose(ka[9], (1, 2, 0, 3)).reshape(model_width, model_width)
+        attn_branch = valid_here * dot_nt(mixed, w_full)[None]
     middle = inputs + attn_branch
     hidden_two, normed_two, inverse_two = normalise(middle, gain_two, shift_two)
     hidden_two_full = gather_tokens(hidden_two.astype(jnp.bfloat16))
@@ -340,6 +876,9 @@
 
 
 def solution(mesh):
+    nf, nt = mesh.shape["fsdp"], mesh.shape["tp"]
+    local = functools.partial(local_layer, nf, nt)
+
     in_specs = (
         P("fsdp", "tp", None),
         P("fsdp", None),

time: 1180 us -> 1180 us (level)
  waiting for transfers between devices: 574 us -> 432 us
  Pallas kernels: 0 us -> 128 us
  starting transfers between devices: 0.94 us -> 13.3 us
    pallas_call x0 -> x1, Pallas kernels: none -> 128 us  [call_ka(): pl.pallas_call(functools.partial(ka_kernel, nf, nt, orders), out_shape=[o...]
    reduce_scatter x2 -> x1, waiting for transfers between devices: 77 us -> 0.01 us  [reduce_tokens(): lax.psum_scatter(values.astype(jnp.bfloat16), 'tp', scatter_dimension=1,...]
    reduce_scatter x2, waiting for transfers between devices: 69.1 us -> 37.9 us  [reduce_grads(): lax.psum_scatter(values.astype(jnp.bfloat16), 'tp', scatter_dimension=1,...]
    all_gather x2, waiting for transfers between devices: 57.5 us -> 28.8 us  [gather_grads(): return lax.all_gather(values, 'tp', axis=1, tiled=True)]
    reduce_scatter x2 -> x1, starting transfers between devices: 0.08 us -> 12.6 us  [reduce_tokens(): lax.psum_scatter(values.astype(jnp.bfloat16), 'tp', scatter_dimension=1,...]
    unnamed x17 -> x16, waiting for transfers between devices: 24.9 us -> 26.8 us
  transfers between devices with their start and end apart: 16 -> 15, of which waited for: 14 -> 10; matrix products, arithmetic and copies ran while one was open for 7% -> 19% of each run, Pallas kernels for 0% -> 11%
where the time goes in v1:
time: 1180 us; the launch traced here: 1170 us
  waiting for transfers between devices  432 us (37%)
  matrix products  224 us (19%)
  blocking collectives  209 us (18%)
  Pallas kernels  128 us (11%)
  other arithmetic  102 us (9%)
  local copies, waits for them, and re-layouts  47.8 us (4%)
  between operations  15.8 us (1%)
  starting transfers between devices  13.3 us (1%)
    pallas_call x1, Pallas kernels, call_ka(): pl.pallas_call(functools.partial(ka_kernel, nf, nt, orders), out_shape=[o...  128 us
    unnamed x2, blocking collectives  82.6 us
    reduce_scatter x1, waiting for transfers between devices, local_layer(): lax.psum_scatter(grad_down, 'fsdp', scatter_dimension=1, tiled=True)  72 us
    reduce_scatter x1, waiting for transfers between devices, local_layer(): lax.psum_scatter(grad_wvalue, 'fsdp', scatter_dimension=0, tiled=True)  65.6 us
    reduce_scatter x1, waiting for transfers between devices, local_layer(): lax.psum_scatter(grad_wkey, 'fsdp', scatter_dimension=0, tiled=True)  65.4 us
    reduce_scatter x1, waiting for transfers between devices, local_layer(): lax.psum_scatter(grad_wquery, 'fsdp', scatter_dimension=0, tiled=True)  65.2 us
    dot_general x8, matrix products, block_scores(): jnp.einsum('qhd,khd->hqk', query, keyed, preferred_element_type=jnp.float32)  39.7 us
    reduce_scatter x2, waiting for transfers between devices, reduce_grads(): lax.psum_scatter(values.astype(jnp.bfloat16), 'tp', scatter_dimension=1,...  37.9 us
  transfers between devices with their start and end apart: 15, of which 10 were waited for; matrix products, arithmetic and copies ran while one was open for 19% of the time, Pallas kernels for 11%

profile of v1, /device:TPU:0, one launch (start us, length us, event | category | flops | bytes accessed | tf_op | source)
XLA Modules:
  0.0 1173.6 jit_solution(15783095762119481108)
XLA Ops:
  19.5 127.5 %shard_map.271 = (bf16[2368,768]{1,0:T(8,128)(2,1)}, f32[2368,192]{1,0:T(8,128)}, f32[2368,192]{1,0:T(8,128)}, bf16[2368,192]{1,0:T(8,128)(2,1)}, bf16[2368,192]...) custom-call(s32[1,4]{1,0:T(1,128)} %lens.1, ...), custom_call_target="tpu_custom_call" | custom-call | tf_op jit(solution)/shard_map/pallas_call | solution.py:520
  152.8 41.8 %all-reduce.14 = (f32[768]{0:T(1024)S(1)}, f32[768]{0:T(1024)S(1)}, f32[768]{0:T(1024)S(1)}, f32[768]{0:T(1024)S(1)}, f32[768]{0:T(1024)S(1)}, /*index=5*/f32[768]{0:T(1024)S(1)}) all-reduce(f32[768]{0:T(1024)S(1)} %dynamic-update-slice.3, f32[768]{0:T(1024)} %copy-done.73, ...), channel_id=1, replica_groups=mesh['fsdp'=8,'tp'=4] {'fsdp','tp'}, use_global_device_ids=true, to_apply=%add.2 | all-reduce | flops 4608 | bytes 36864
  195.1 3.6 fusion.128
  203.8 25.8 %all-gather.7.cloned.1.call-done = bf16[1,2048,768]{2,1,0:T(8,128)(2,1)} async-done(((bf16[1,512,768]{2,1,0:T(8,128)(2,1)}), bf16[1,2048,768]{2,1,0:T(8,128)(2,1)}) %all-gather.7.cloned.1.call-update) | async-done | bytes 3145744 | tf_op jit(solution)/shard_map/all_gather | solution.py:564
  229.6 18.2 %fusion.47 = (bf16[2048,768]{1,0:T(8,128)(2,1)}, f32[2048,768]{1,0:T(8,128)}) fusion(bf16[768,768]{1,0:T(8,128)(2,1)} %all-gather.9.cloned.1.call-done, bf16[1,2048,768]{2,1,0:T(8,128)(2,1)} %all-gather.7.cloned.1.call-done), kind=kOutput, calls=%fused_computation.61 | convolution fusion | flops 2518155264 | bytes 13762560 | tf_op jit(solution)/shard_map/dot_general | solution.py:743
  247.9 25.0 %all-gather.11.cloned.1.call-done = bf16[768,768]{0,1:T(8,128)(2,1)} async-done(((bf16[768,96]{0,1:T(8,128)(2,1)}), bf16[768,768]{0,1:T(8,128)(2,1)}) %all-gather.11.cloned.1.call-update) | async-done | bytes 1179664 | tf_op jit(solution)/shard_map/all_gather | solution.py:741
  272.9 28.8 %all-gather.13.cloned.1.call-done = bf16[1,2048,768]{2,1,0:T(8,128)(2,1)} async-done(((bf16[1,512,768]{2,1,0:T(8,128)(2,1)}), bf16[1,2048,768]{2,1,0:T(8,128)(2,1)}) %all-gather.13.cloned.1.call-update) | async-done | bytes 3145744 | tf_op jit(solution)/shard_map/all_gather | solution.py:568
  301.7 6.7 fusion.53
  310.0 4.0 fusion.85
  314.1 12.6 %reduce-scatter.12.cloned.1.call-start = ((), (), s32[]{:S(2)}) async-start(), calls=%async_computation.12 | async-start | bytes 3932160 | tf_op jit(solution)/shard_map/reduce_scatter | solution.py:572
  326.6 6.2 fusion.84
  335.1 31.2 %all_gather.62 = bf16[768,192]{1,0:T(8,128)(2,1)S(1)} all-gather(bf16[96,192]{1,0:T(8,128)(2,1)S(1)} %copy-done.47), channel_id=1, replica_groups=mesh['fsdp'=8,'tp'=4] {'fsdp'}, dimensions={0}, use_global_device_ids=true | all-gather | bytes 331776 | tf_op jit(solution)/shard_map/all_gather | solution.py:700
  366.3 31.3 %all_gather.64 = bf16[768,192]{1,0:T(8,128)(2,1)S(1)} all-gather(bf16[96,192]{1,0:T(8,128)(2,1)S(1)} %copy-done.48), channel_id=1, replica_groups=mesh['fsdp'=8,'tp'=4] {'fsdp'}, dimensions={0}, use_global_device_ids=true | all-gather | bytes 331776 | tf_op jit(solution)/shard_map/all_gather | solution.py:701
  397.5 31.1 %all_gather.66 = bf16[768,192]{1,0:T(8,128)(2,1)S(1)} all-gather(bf16[96,192]{1,0:T(8,128)(2,1)S(1)} %copy-done.49), channel_id=1, replica_groups=mesh['fsdp'=8,'tp'=4] {'fsdp'}, dimensions={0}, use_global_device_ids=true | all-gather | bytes 331776 | tf_op jit(solution)/shard_map/all_gather | solution.py:702
  428.6 33.2 %all_gather.68 = bf16[192,768]{0,1:T(8,128)(2,1)} all-gather(bf16[192,96]{0,1:T(8,128)(2,1)S(1)} %copy-done.46), channel_id=1, replica_groups=mesh['fsdp'=8,'tp'=4] {'fsdp'}, dimensions={1}, use_global_device_ids=true | all-gather | bytes 331776 | tf_op jit(solution)/shard_map/all_gather | solution.py:766
  462.7 3.1 fusion.75
  468.2 3.1 fusion.73
  479.0 3.4 fusion.114
  482.4 4.6 multiply_convert_fusion.2
  487.1 88.9 %while.51 = (s32[]{:T(128)}, bf16[4,512,3,64]{1,3,2,0:T(8,128)(2,1)S(1)}, f32[4,3,512,1]{2,1,3,0:T(4,128)}, s32[4,512]{1,0:T(4,128)S(1)}, s32[2048]{0:T(1024)S(1...) while((s32[]{:T(128)}, ...), condition=%wide.region_16.17_spmd.clone.clone, body=%wide.region_13.16_spmd.clone.sunk.clone | while | flops 842011136 | bytes 44177528 | solution.py:607
  488.5 7.3 fusion.198
  495.8 6.8 exponential_reduce_fusion.3
  503.2 6.5 fusion.199
  511.2 6.8 fusion.198
  518.0 6.8 exponential_reduce_fusion.3
  525.4 6.4 fusion.199
  533.3 6.8 fusion.198
  540.1 6.8 exponential_reduce_fusion.3
  547.4 6.4 fusion.199
  555.3 6.8 fusion.198
  562.1 6.8 exponential_reduce_fusion.3
  569.5 6.4 fusion.199
  577.7 3.1 fusion.90
  581.5 132.8 %while.52 = (s32[]{:T(128)}, f32[2048,3,64]{0,2,1:T(8,128)}, f32[2048,3,64]{0,2,1:T(8,128)}, f32[4,512,3,64]{1,3,2,0:T(8,128)}, bf16[4,512,3,64]{1,3,2,0:T(8,128...) while((s32[]{:T(128)}, f32[2048,3,64]{0,2,1:T(8,128)}, ...), condition=%wide.region_19.20_spmd.clone.clone, body=%wide.region_17.19_spmd.clone.sunk.clone | while | flops 2064617984 | bytes 169277904 | solution.py:641
  587.2 4.7 fusion.211
  591.9 5.8 multiply_reduce_fusion.14
  597.7 4.9 multiply_convert_fusion.7
  607.8 6.2 fusion.212
  619.2 6.1 fusion.211
  625.4 5.8 multiply_reduce_fusion.14
  631.1 4.9 multiply_convert_fusion.7
  641.2 6.2 fusion.212
  652.6 6.1 fusion.211
  658.8 5.8 multiply_reduce_fusion.14
  664.5 4.9 multiply_convert_fusion.7
  674.6 6.2 fusion.212
  686.0 6.1 fusion.211
  692.2 5.8 multiply_reduce_fusion.14
  697.9 4.9 multiply_convert_fusion.7
  708.0 6.2 fusion.212
  714.4 3.1 multiply_reduce_fusion.4
  733.7 6.0 fusion.80
  740.0 7.2 fusion.77
  750.4 3.0 fusion.65
  757.7 3.1 fusion.69
  760.9 24.7 %reduce-scatter.28.cloned.1.call-done = f32[96,192]{1,0:T(8,128)} async-done(((f32[768,192]{1,0:T(8,128)}), f32[96,192]{1,0:T(8,128)}) %reduce-scatter.28.cloned.1.call-update) | async-done | bytes 73744
  787.2 37.8 %reduce-scatter.16.cloned.1.call-done = bf16[1,512,768]{2,1,0:T(8,128)(2,1)} async-done(((bf16[1,2048,768]{2,1,0:T(8,128)(2,1)}), bf16[1,512,768]{2,1,0:T(8,128)(2,1)}) %reduce-scatter.16.cloned.1.call-update) | async-done | bytes 786448 | tf_op jit(solution)/shard_map/reduce_scatter | solution.py:578
  825.0 3.1 fusion.115
  830.8 40.8 %all-reduce.13 = (f32[768]{0:T(1024)S(1)}, f32[768]{0:T(1024)S(1)}, f32[768]{0:T(1024)S(1)}, f32[768]{0:T(1024)S(1)}, f32[768]{0:T(1024)S(1)}, /*index=5*/f32[768]{0:T(1024)S(1)}, f32[4]{0:T(128)S(1)}, f32[]{:T(128)}) all-reduce(f32[768]{0:T(1024)S(1)} %get-tuple-element.322, ...), channel_id=11, replica_groups=mesh['fsdp'=8,'tp'=4] {'fsdp','tp'}, use_global_device_ids=true, to_apply=%region_34.35.clone | all-reduce | flops 4613 | bytes 36904
  879.1 19.6 %reduce-scatter.24.cloned.1.call-done = f32[96,768]{1,0:T(8,128)} async-done(((f32[768,768]{1,0:T(8,128)}), f32[96,768]{1,0:T(8,128)}) %reduce-scatter.24.cloned.1.call-update) | async-done | bytes 294928 | tf_op jit(solution)/shard_map/reduce_scatter | solution.py:780
  898.7 72.0 %reduce-scatter.26.cloned.1.call-done = f32[768,96]{0,1:T(8,128)} async-done(((f32[768,768]{0,1:T(8,128)}), f32[768,96]{0,1:T(8,128)}) %reduce-scatter.26.cloned.1.call-update) | async-done | bytes 294928 | tf_op jit(solution)/shard_map/reduce_scatter | solution.py:781
  970.7 65.4 %reduce-scatter.20.cloned.1.call-done = f32[96,192]{1,0:T(8,128)} async-done(((f32[768,192]{1,0:T(8,128)}), f32[96,192]{1,0:T(8,128)}) %reduce-scatter.20.cloned.1.call-update) | async-done | bytes 73744 | tf_op jit(solution)/shard_map/reduce_scatter | solution.py:834
  1036.1 65.6 %reduce-scatter.22.cloned.1.call-done = f32[96,192]{1,0:T(8,128)} async-done(((f32[768,192]{1,0:T(8,128)}), f32[96,192]{1,0:T(8,128)}) %reduce-scatter.22.cloned.1.call-update) | async-done | bytes 73744 | tf_op jit(solution)/shard_map/reduce_scatter | solution.py:835
  1101.7 65.2 %reduce-scatter.18.cloned.1.call-done = f32[96,192]{1,0:T(8,128)} async-done(((f32[768,192]{1,0:T(8,128)}), f32[96,192]{1,0:T(8,128)}) %reduce-scatter.18.cloned.1.call-update) | async-done | bytes 73744 | tf_op jit(solution)/shard_map/reduce_scatter | solution.py:833
  (388 shorter events, 124.7 us)
Async XLA Ops:
  7.2 196.7 %all-gather.9.cloned.1.call-start = ((), (), s32[]{:S(2)}) async-start(), calls=%async_computation.10 | async-start | bytes 1327104 | tf_op jit(solution)/shard_map/all_gather | solution.py:740
  7.9 221.7 %all-gather.7.cloned.1.call-start = ((), (), s32[]{:S(2)}) async-start(), calls=%async_computation.9 | async-start | bytes 3932160 | tf_op jit(solution)/shard_map/all_gather | solution.py:564
  11.5 190.5 %copy-start.50 = (f32[1,512]{1,0:T(1,128)}, f32[1,512]{1,0:T(1,128)S(1)}, u32[]{:S(2)}) copy-start(f32[1,512]{1,0:T(1,128)S(1)} %compare_convert_fusion) | copy-start | bytes 6148
  17.3 129.7 %copy-start.73 = (f32[768]{0:T(1024)}, f32[768]{0:T(1024)S(1)}, u32[]{:S(2)}) copy-start(f32[768]{0:T(1024)S(1)} %dynamic-update-slice.2) | copy-start | bytes 9220
  149.2 45.4 %copy-start.16 = (bf16[1,512,768]{2,1,0:T(8,128)(2,1)S(1)}, bf16[1,512,768]{2,1,0:T(8,128)(2,1)}, u32[]{:S(2)}) copy-start(bf16[1,512,768]{2,1,0:T(8,128)(2,1)} %param.22) | copy-start | bytes 2359300
  201.2 71.7 %all-gather.11.cloned.1.call-start = ((), (), s32[]{:S(2)}) async-start(), calls=%async_computation.11 | async-start | bytes 1327104 | tf_op jit(solution)/shard_map/all_gather | solution.py:741
  201.9 99.7 %all-gather.13.cloned.1.call-start = ((), (), s32[]{:S(2)}) async-start(), calls=%async_computation.13 | async-start | bytes 3932160 | tf_op jit(solution)/shard_map/all_gather | solution.py:568
  203.2 259.6 %all-gather.15.cloned.1.call-start = ((), (), s32[]{:S(2)}) async-start(), calls=%async_computation.15 | async-start | bytes 3932160 | tf_op jit(solution)/shard_map/all_gather | solution.py:564
  203.8 275.2 %reduce-scatter.14.cloned.1.call-start = ((), (), s32[]{:S(2)}) async-start(), calls=%async_computation.14 | async-start | bytes 3932160 | tf_op jit(solution)/shard_map/reduce_scatter | solution.py:578
  301.6 8.4 copy-start.77
  314.0 12.6 %copy-start.78 = (bf16[768,768]{0,1:T(8,128)(2,1)S(1)}, bf16[768,768]{0,1:T(8,128)(2,1)}, u32[]{:S(2)}) copy-start(bf16[768,768]{0,1:T(8,128)(2,1)} %all-gather.11.cloned.1.call-done) | copy-start | bytes 3538948
  314.1 168.3 %reduce-scatter.12.cloned.1.call-start = ((), (), s32[]{:S(2)}) async-start(), calls=%async_computation.12 | async-start | bytes 3932160 | tf_op jit(solution)/shard_map/reduce_scatter | solution.py:572
  332.8 33.4 %copy-start.48 = (bf16[96,192]{1,0:T(8,128)(2,1)S(1)}, bf16[96,192]{1,0:T(8,128)(2,1)}, u32[]{:S(2)}) copy-start(bf16[96,192]{1,0:T(8,128)(2,1)} %param.26) | copy-start | bytes 110596
  332.8 64.7 %copy-start.49 = (bf16[96,192]{1,0:T(8,128)(2,1)S(1)}, bf16[96,192]{1,0:T(8,128)(2,1)}, u32[]{:S(2)}) copy-start(bf16[96,192]{1,0:T(8,128)(2,1)} %param.27) | copy-start | bytes 110596
  332.8 95.7 %copy-start.46 = (bf16[192,96]{0,1:T(8,128)(2,1)S(1)}, bf16[192,96]{0,1:T(8,128)(2,1)}, u32[]{:S(2)}) copy-start(bf16[192,96]{0,1:T(8,128)(2,1)} %copy.50) | copy-start | bytes 110596
  332.9 244.8 %all-gather.17.cloned.1.call-start = ((), (), s32[]{:S(2)}) async-start(), calls=%async_computation.16 | async-start | bytes 3932160 | tf_op jit(solution)/shard_map/all_gather | solution.py:568
  333.9 140.0 %copy-start.67 = (f32[3,64]{1,0:T(4,128)}, f32[3,64]{1,0:T(4,128)S(1)}, u32[]{:S(2)}) copy-start(f32[3,64]{1,0:T(4,128)S(1)} %mul.435) | copy-start | bytes 2308
  366.3 99.5 %copy-start.27 = (bf16[768,192]{1,0:T(8,128)(2,1)}, bf16[768,192]{1,0:T(8,128)(2,1)S(1)}, u32[]{:S(2)}) copy-start(bf16[768,192]{1,0:T(8,128)(2,1)S(1)} %all_gather.62) | copy-start | bytes 884740
  397.5 70.7 %copy-start.25 = (bf16[768,192]{1,0:T(8,128)(2,1)}, bf16[768,192]{1,0:T(8,128)(2,1)S(1)}, u32[]{:S(2)}) copy-start(bf16[768,192]{1,0:T(8,128)(2,1)S(1)} %all_gather.64) | copy-start | bytes 884740
  428.6 48.8 %copy-start.29 = (bf16[768,192]{1,0:T(8,128)(2,1)}, bf16[768,192]{1,0:T(8,128)(2,1)S(1)}, u32[]{:S(2)}) copy-start(bf16[768,192]{1,0:T(8,128)(2,1)S(1)} %all_gather.66) | copy-start | bytes 884740
  471.3 7.3 copy-start.7
  471.4 6.0 copy-start.14
  478.7 8.3 copy-start.44
  487.0 298.5 %reduce-scatter.28.cloned.1.call-start = ((), (), s32[]{:S(2)}) async-start(), calls=%async_computation.23 | async-start | bytes 884736
  581.5 132.9 %copy-start.38 = (f32[2048,3]{0,1:T(4,128)S(1)}, f32[2048,3]{0,1:T(4,128)}, u32[]{:S(2)}) copy-start(f32[2048,3]{0,1:T(4,128)} %copy-done.37) | copy-start | bytes 73732
  581.5 132.9 %copy-start.43 = (f32[2048,3]{0,1:T(4,128)S(1)}, f32[2048,3]{0,1:T(4,128)}, u32[]{:S(2)}) copy-start(f32[2048,3]{0,1:T(4,128)} %copy-done.42) | copy-start | bytes 73732
  581.5 132.9 %copy-start.68 = (f32[3,64]{1,0:T(4,128)S(1)}, f32[3,64]{1,0:T(4,128)}, u32[]{:S(2)}) copy-start(f32[3,64]{1,0:T(4,128)} %copy-done.67) | copy-start | bytes 2308
  597.7 7.6 copy-start.4
  607.7 6.2 copy-start.5
  607.7 6.2 copy-start.10
  607.7 6.2 copy-start.24
  614.0 5.2 copy-start.2
  614.0 5.2 copy-start.9
  614.0 5.2 copy-start.23
  631.1 7.6 copy-start.4
  641.1 6.2 copy-start.5
  641.1 6.2 copy-start.10
  641.2 6.2 copy-start.24
  664.5 7.6 copy-start.4
  674.5 6.2 copy-start.5
  674.5 6.2 copy-start.10
  674.6 6.2 copy-start.24
  680.8 5.2 copy-start.2
  680.8 5.2 copy-start.9
  680.8 5.2 copy-start.23
  697.9 7.6 copy-start.4
  708.0 6.2 copy-start.5
  708.0 6.2 copy-start.10
  708.0 6.2 copy-start.24
  722.7 102.3 %reduce-scatter.16.cloned.1.call-start = ((), (), s32[]{:S(2)}) async-start(), calls=%async_computation.17 | async-start | bytes 3932160 | tf_op jit(solution)/shard_map/reduce_scatter | solution.py:578
  731.9 166.8 %reduce-scatter.24.cloned.1.call-start = ((), (), s32[]{:S(2)}) async-start(), calls=%async_computation.21 | async-start | bytes 2654208 | tf_op jit(solution)/shard_map/reduce_scatter | solution.py:780
  739.7 7.5 copy-start.15
  739.7 230.9 %reduce-scatter.26.cloned.1.call-start = ((), (), s32[]{:S(2)}) async-start(), calls=%async_computation.22 | async-start | bytes 2654208 | tf_op jit(solution)/shard_map/reduce_scatter | solution.py:781
  747.2 288.9 %reduce-scatter.20.cloned.1.call-start = ((), (), s32[]{:S(2)}) async-start(), calls=%async_computation.19 | async-start | bytes 884736 | tf_op jit(solution)/shard_map/reduce_scatter | solution.py:834
  750.3 351.4 %reduce-scatter.22.cloned.1.call-start = ((), (), s32[]{:S(2)}) async-start(), calls=%async_computation.20 | async-start | bytes 884736 | tf_op jit(solution)/shard_map/reduce_scatter | solution.py:835
  753.4 413.4 %reduce-scatter.18.cloned.1.call-start = ((), (), s32[]{:S(2)}) async-start(), calls=%async_computation.18 | async-start | bytes 884736 | tf_op jit(solution)/shard_map/reduce_scatter | solution.py:833
  757.7 67.3 %copy-start.52 = (f32[1,512]{1,0:T(1,128)S(1)}, f32[1,512]{1,0:T(1,128)}, u32[]{:S(2)}) copy-start(f32[1,512]{1,0:T(1,128)} %copy-done.50) | copy-start | bytes 6148
  757.7 67.3 %copy-start.54 = (f32[512]{0:T(512)S(1)}, f32[512]{0:T(512)}, u32[]{:S(2)}) copy-start(f32[512]{0:T(512)} %copy-done.53) | copy-start | bytes 6148
  757.7 67.3 %copy-start.60 = (f32[768]{0:T(1024)S(1)}, f32[768]{0:T(1024)}, u32[]{:S(2)}) copy-start(f32[768]{0:T(1024)} %copy-done.59) | copy-start | bytes 9220
  757.7 67.3 %copy-start.62 = (f32[512]{0:T(512)S(1)}, f32[512]{0:T(512)}, u32[]{:S(2)}) copy-start(f32[512]{0:T(512)} %copy-done.61) | copy-start | bytes 6148
  757.7 73.1 %copy-start.69 = (f32[768]{0:T(1024)S(1)}, f32[768]{0:T(1024)}, u32[]{:S(2)}) copy-start(f32[768]{0:T(1024)} %get-tuple-element.320) | copy-start | bytes 9220
  757.7 73.1 %copy-start.70 = (f32[768]{0:T(1024)S(1)}, f32[768]{0:T(1024)}, u32[]{:S(2)}) copy-start(f32[768]{0:T(1024)} %get-tuple-element.329) | copy-start | bytes 9220
  760.8 115.5 %copy-start.17 = (bf16[1,512,768]{2,1,0:T(8,128)(2,1)S(1)}, bf16[1,512,768]{2,1,0:T(8,128)(2,1)}, u32[]{:S(2)}) copy-start(bf16[1,512,768]{2,1,0:T(8,128)(2,1)} %param.22) | copy-start | bytes 2359300
  760.8 115.5 %copy-start.20 = (f32[1,512,768]{2,1,0:T(8,128)S(1)}, f32[1,512,768]{2,1,0:T(8,128)}, u32[]{:S(2)}) copy-start(f32[1,512,768]{2,1,0:T(8,128)} %get-tuple-element.391) | copy-start | bytes 4718596
  (61 other events, 174.7 us)
Sparse Core Ops, SparseCore 0:
  10.2 62.4 all-gather.8
  201.3 28.2 all-gather.6
  231.8 41.0 all-gather.10
  274.3 27.2 all-gather.12
  303.1 28.5 all-gather.14
  334.0 37.9 reduce-scatter.13
  374.7 37.9 reduce-scatter.11
  487.1 28.4 all-gather.16
  722.8 62.6 reduce-scatter.27
  788.1 36.8 reduce-scatter.15
  829.1 69.5 reduce-scatter.23
  902.6 68.0 reduce-scatter.25
  974.5 61.5 reduce-scatter.19
  1040.2 61.4 reduce-scatter.21
  1105.4 61.3 reduce-scatter.17
